TPU v7x, 256 devices: a whole 4x4x8 slice. The times are simulated.
256 devices in a mesh: branch: 2 (over y_lo), seq: 16 (over z, core), mp: 8 (over x, y_hi).
Axes of the slice: x: 4, y: 4 (y_hi: 2, y_lo: 2; y = y_hi * 2 + y_lo), z: 8, core: 2. Of those that a mesh axis runs over, the one named last changes fastest.
Arguments:
- queries: bfloat16 [2, 16, 2048, 2048], P('branch', 'mp', 'seq'), may hold values from -8 to 8
- keys: bfloat16 [2, 16, 2048, 2048], P('branch', 'mp', 'seq'), may hold values from -8 to 8
- values: bfloat16 [2, 16, 2048, 2048], P('branch', 'mp', 'seq'), may hold values from -6 to 6
- inject: float32 [2, 16], P('branch'), may hold values from 0.2 to 0.8
- keyframes: int32 [2], replicated, may hold values from 0 to 15, as said below
- key_mask: int32 [16, 2], replicated, may hold values 0 or 1
Outputs:
- attended: bfloat16 [2, 16, 2048, 2048], P('branch', 'mp', 'seq')
Inputs may be any that keep to these rules, and one draw needn't show every extreme that they name: The keyframes are distinct frames; one of them is the last frame.
All inputs are finite; a program needn't handle non-finite values.
Results may differ from a plain program's by a relative error of at most 0.0061.
Values may be sent and summed in bfloat16 or wider, within the bound.
No kernel may reach another device: no remote copies, remote signals or barrier semaphores. Data moves between devices by JAX's collectives and lax.ppermute only.
A program may use at most 64 MiB of HBM per device.

v0:
```python
import math
import jax
import jax.numpy as jnp
from jax import lax
from jax.sharding import PartitionSpec as P

HEAD = 128
NEG_FILL = -1e30


def swapped(value, axis, bit):
    mask = 2**bit
    pairs = [(source, source ^ mask) for source in range(lax.axis_size(axis))]
    return lax.ppermute(value, axis, pairs)


def from_root(block, axis, holder):
    block = jnp.where(lax.axis_index(axis) == holder, block, jnp.zeros_like(block))
    return lax.psum(block, axis)


def blend_pair(source, partner, strength):
    return (
        (1.0 - strength) * source.astype(jnp.float32) + strength * partner.astype(jnp.float32)
    ).astype(jnp.bfloat16)


def score_tile(query_block, key_tile):
    return jnp.einsum("qhd,khd->hqk", query_block, key_tile, preferred_element_type=jnp.float32) * (
        1.0 / math.sqrt(HEAD)
    )


def attend_frame(query_rows, key_own, value_own, key_extra, value_extra, mask_row):
    frame_rows = query_rows.shape[0]
    row_width = query_rows.shape[1]
    local_heads = row_width // HEAD
    rows_block = min(512, frame_rows)
    key_count = key_extra.shape[0]
    split_queries = query_rows.reshape(frame_rows // rows_block, rows_block, local_heads, HEAD)
    key_own = key_own.reshape(frame_rows, local_heads, HEAD)
    value_own = value_own.reshape(frame_rows, local_heads, HEAD)
    key_extra = key_extra.reshape(key_count, frame_rows, local_heads, HEAD)
    value_extra = value_extra.reshape(key_count, frame_rows, local_heads, HEAD)
    present = mask_row > 0
    valid_keys = jnp.concatenate(
        [jnp.ones((frame_rows,), jnp.bool_), jnp.repeat(present, frame_rows)]
    )
    key_whole = jnp.concatenate(
        [key_own, key_extra.reshape(key_count * frame_rows, local_heads, HEAD)], axis=0
    )
    value_whole = jnp.concatenate(
        [value_own, value_extra.reshape(key_count * frame_rows, local_heads, HEAD)], axis=0
    )

    def one_block(query_block):
        scores = score_tile(query_block, key_whole)
        scores = jnp.where(valid_keys[None, None, :], scores, NEG_FILL)
        row_max = jnp.max(scores, axis=2, keepdims=True)
        weights = jnp.where(valid_keys[None, None, :], jnp.exp(scores - row_max), 0.0)
        totals = jnp.sum(weights, axis=2)
        rounded = weights.astype(jnp.bfloat16)
        mixed_out = jnp.einsum(
            "hqk,khd->qhd", rounded, value_whole, preferred_element_type=jnp.float32
        )
        result = mixed_out / jnp.transpose(totals)[:, :, None]
        return result.reshape(rows_block, row_width).astype(jnp.bfloat16)

    return lax.map(one_block, split_queries).reshape(frame_rows, row_width)


def local(queries, keys, values, inject, keyframes, key_mask):
    frames_dev = queries.shape[1]
    total_heads = inject.shape[1]
    strength = jnp.repeat(inject[0], HEAD, total_repeat_length=total_heads * HEAD)
    partner_queries, partner_keys = swapped((queries, keys), "branch", 0)
    mixed_queries = blend_pair(queries, partner_queries, strength)
    mixed_keys = blend_pair(keys, partner_keys, strength)
    head_queries, head_keys, head_values = (
        lax.all_to_all(mixed_queries, "seq", split_axis=3, concat_axis=2, tiled=True),
        lax.all_to_all(mixed_keys, "seq", split_axis=3, concat_axis=2, tiled=True),
        lax.all_to_all(values, "seq", split_axis=3, concat_axis=2, tiled=True),
    )
    frame_keys = head_keys[0]
    frame_values = head_values[0]
    mp_index = lax.axis_index("mp")
    extra_keys = []
    extra_values = []
    for keyframe_slot in range(keyframes.shape[0]):
        chosen = keyframes[keyframe_slot]
        local_slot = chosen % frames_dev
        chosen_key = lax.dynamic_index_in_dim(frame_keys, local_slot, 0, keepdims=False)
        chosen_value = lax.dynamic_index_in_dim(frame_values, local_slot, 0, keepdims=False)
        got_key, got_value = (
            from_root(chosen_key, "mp", chosen // frames_dev),
            from_root(chosen_value, "mp", chosen // frames_dev),
        )
        extra_keys.append(got_key)
        extra_values.append(got_value)
    key_extra = jnp.stack(extra_keys)
    value_extra = jnp.stack(extra_values)
    outputs = []
    for local_frame in range(frames_dev):
        mask_row = lax.dynamic_index_in_dim(
            key_mask, mp_index * frames_dev + local_frame, 0, keepdims=False
        )
        outputs.append(
            attend_frame(
                head_queries[0, local_frame],
                frame_keys[local_frame],
                frame_values[local_frame],
                key_extra,
                value_extra,
                mask_row,
            )
        )
    attended = jnp.stack(outputs)[None]
    return lax.all_to_all(attended, "seq", split_axis=2, concat_axis=3, tiled=True)


def solution(mesh):
    return jax.shard_map(
        local,
        mesh=mesh,
        in_specs=(
            P("branch", "mp", "seq", None),
            P("branch", "mp", "seq", None),
            P("branch", "mp", "seq", None),
            P("branch", None),
            P(),
            P(),
        ),
        out_specs=P("branch", "mp", "seq", None),
        check_vma=False,
    )
```

profile of v0, /device:TPU:1, one launch (start us, length us, event | category | flops | bytes accessed | tf_op | source)
XLA Modules:
  0.0 387.3 jit_solution(7415376909329658251)
XLA Ops:
  6.5 3.7 copy.89
  10.2 10.0 %all-to-all-start.2 = ((bf16[1,2,128,2048]{2,1,0,3:T(2,128)(2,1)}), bf16[1,2,128,2048]{2,1,0,3:T(2,128)(2,1)S(1)}, u32[]{:S(2)}, u32[]{:S(2)}) async-start(bf16[1,2,128,2048]{2,1,0,3:T(2,128)(2,1)} %copy.89), calls=%async_computation.2 | async-start | bytes 2097152 | tf_op jit(solution)/shard_map/all_to_all | solution.py:82
  20.2 1.3 collective-permute-start
  21.6 1.9 fusion.86
  23.6 4.3 %compare_select_fusion.1 = (f32[2048,1]{0,1:T(1,128)S(1)}, s32[2048,1]{0,1:T(1,128)S(1)}) fusion(f32[]{:T(128)} %bitcast.27, f32[]{:T(128)} %bitcast.28, f32[]{:T(128)} %bitcast.29, f32[]{:T(128)} %bitcast.30, f32[]{:T(128)} %bitcast.31, f32[]{:T(128)} %bitcast.33, f32[]{:T(128)} %bitcast.32, s32[2048,1]{0,1:T(1,128)S(1)} %bitcast.185, ...), kind=kLoop, calls=%fused_computation.65 | loop fusion | flops 28672 | bytes 32796 | tf_op jit(solution)/shard_map/jit(_take)/gather | solution.py:75
  28.1 5.7 %broadcast_subtract_fusion = (f32[2048]{0:T(1024)S(1)}, f32[2048]{0:T(1024)S(1)}) fusion(pred[2048]{0:T(1024)(128)(4,1)S(1)} %get-tuple-element.163, pred[2048]{0:T(1024)(128)(4,1)S(1)} %get-tuple-element.162, pred[2048]{0:T(1024)(128)(4,1)S(1)} %get-tuple-element.161, pred[2048]{0:T(1024)(128)(4,1)S(1)} %get-tuple-element.160, ...), kind=kLoop, calls=%fused_computation.76 | loop fusion | flops 38912 | bytes 43044 | tf_op jit(solution)/shard_map/sub | solution.py:24
  33.8 11.1 %collective-permute-done = bf16[1,2,128,2048]{3,2,1,0:T(8,128)(2,1)S(1)} collective-permute-done((bf16[1,2,128,2048]{3,2,1,0:T(8,128)(2,1)}, bf16[1,2,128,2048]{3,2,1,0:T(8,128)(2,1)S(1)}, u32[]{:S(2)}, u32[]{:S(2)}) %collective-permute-start) | collective-permute-done | bytes 1048608 | tf_op jit(solution)/shard_map/ppermute | solution.py:14
  44.9 22.5 %collective-permute-done.1 = bf16[1,2,128,2048]{3,2,1,0:T(8,128)(2,1)S(1)} collective-permute-done((bf16[1,2,128,2048]{3,2,1,0:T(8,128)(2,1)}, bf16[1,2,128,2048]{3,2,1,0:T(8,128)(2,1)S(1)}, u32[]{:S(2)}, u32[]{:S(2)}) %collective-permute-start.1) | collective-permute-done | bytes 1048608 | tf_op jit(solution)/shard_map/ppermute | solution.py:14
  67.4 2.4 add_convert_fusion
  69.8 2.0 copy.85
  71.8 7.9 %all-to-all-start.1 = ((bf16[1,2,128,2048]{2,1,0,3:T(2,128)(2,1)}), bf16[1,2,128,2048]{2,1,0,3:T(2,128)(2,1)S(1)}, u32[]{:S(2)}, u32[]{:S(2)}) async-start(bf16[1,2,128,2048]{2,1,0,3:T(2,128)(2,1)} %copy.85), calls=%async_computation.1 | async-start | bytes 2097152 | tf_op jit(solution)/shard_map/all_to_all | solution.py:81
  79.7 2.0 copy.83
  81.7 26.0 %all-to-all-done.1 = bf16[1,2,128,2048]{2,1,0,3:T(2,128)(2,1)S(1)} async-done(((bf16[1,2,128,2048]{2,1,0,3:T(2,128)(2,1)}), bf16[1,2,128,2048]{2,1,0,3:T(2,128)(2,1)S(1)}, u32[]{:S(2)}, u32[]{:S(2)}) %all-to-all-start.1) | async-done | bytes 1048608 | tf_op jit(solution)/shard_map/all_to_all | solution.py:81
  107.7 1.0 copy-done
  108.7 3.6 all-to-all-start
  118.3 1.3 copy.92
  119.7 1.4 copy.86
  121.0 1.3 copy.88
  122.4 2.9 dynamic-slice_select_fusion.1
  125.8 1.1 fusion.82
  126.8 1.3 copy.91
  128.2 1.3 copy.95
  129.5 1.1 fusion.83
  130.5 2.1 copy.87
  132.6 2.1 copy.94
  134.7 5.5 %all-to-all-done = bf16[1,2,128,2048]{2,1,0,3:T(2,128)(2,1)S(1)} async-done(((bf16[1,2,128,2048]{2,1,0,3:T(2,128)(2,1)}), bf16[1,2,128,2048]{2,1,0,3:T(2,128)(2,1)S(1)}, u32[]{:S(2)}, u32[]{:S(2)}) %all-to-all-start) | async-done | bytes 1048608 | tf_op jit(solution)/shard_map/all_to_all | solution.py:80
  140.1 0.9 copy.84
  141.1 1.0 fusion.84
  142.1 97.8 %all-reduce.5.cloned.1.call-done = (bf16[1,2048,128]{2,1,0:T(8,128)(2,1)}, bf16[1,2048,128]{2,1,0:T(8,128)(2,1)}, bf16[1,2048,128]{2,1,0:T(8,128)(2,1)}, bf16[1,2048,128]{2,1,0:T(8,128)(2,1)}) async-done(((bf16[1,2048,128]{2,1,0:T(8,128)(2,1)}, bf16[1,2048,128]{2,1,0:T(8,128)(2,1)}, bf16[1,2048,128]{2,1,0:T(8,128)(2,1)}, bf16[1,2048,128]{2,1,0:T(8,128)(2,1)}), (bf16[1,2048,128]{2,1,0:T(8,128)(2,1)}, ...) | async-done | bytes 2097168 | tf_op jit(solution)/shard_map/psum | solution.py:19
  239.9 1.4 pad_maximum_fusion.5
  241.3 1.3 pad_maximum_fusion.4
  242.6 1.9 pad_maximum_fusion.3
  244.7 0.9 broadcast.203.clone.1
  245.6 42.6 %while.21 = (s32[]{:T(128)}, bf16[4,512,128]{2,1,0:T(8,128)(2,1)}, pred[6144]{0:T(1024)(128)(4,1)S(1)}, bf16[4,512,1,128]{3,1,2,0:T(8,128)(2,1)}, bf16[6144,1,12...) while((s32[]{:T(128)}, bf16[4,512,128]{2,1,0:T(8,128)(2,1)}, ...), condition=%wide.region_7.8_spmd, body=%wide.region_4.7_spmd.sunk | while | flops 1651637248 | bytes 47477864 | solution.py:69
  245.6 3.0 fusion.99
  248.6 3.3 fusion.100
  251.9 4.3 %fusion.101 = bf16[4,512,128]{2,1,0:T(8,128)(2,1)} fusion(bf16[4,512,128]{2,1,0:T(8,128)(2,1)} %get-tuple-element.349, s32[]{:T(128)} %get-tuple-element.348, bf16[6144,1,128]{2,0,1:T(8,128)(2,1)S(1)} %copy-done.4, f32[512,6144]{1,0:T(8,128)S(1)} %get-tuple-element.310, f32[512]{0:T(512)S(1)} %get-tuple-element.311, ...), kind=kOutput, calls=%fused_computation.14.clone.1 | convolution fusion | flops 821166080 | bytes 14297600 | tf_op jit(solution)/shard_map/while/body/eval_jaxpr/hqk,khd->qhd/dot_general | solution.py:63
  256.2 3.0 fusion.99
  259.3 3.3 fusion.100
  262.6 4.3 %fusion.101 = bf16[4,512,128]{2,1,0:T(8,128)(2,1)} fusion(bf16[4,512,128]{2,1,0:T(8,128)(2,1)} %get-tuple-element.349, s32[]{:T(128)} %get-tuple-element.348, bf16[6144,1,128]{2,0,1:T(8,128)(2,1)S(1)} %copy-done.4, f32[512,6144]{1,0:T(8,128)S(1)} %get-tuple-element.310, f32[512]{0:T(512)S(1)} %get-tuple-element.311, ...), kind=kOutput, calls=%fused_computation.14.clone.1 | convolution fusion | flops 821166080 | bytes 14297600 | tf_op jit(solution)/shard_map/while/body/eval_jaxpr/hqk,khd->qhd/dot_general | solution.py:63
  266.9 3.0 fusion.99
  269.9 3.3 fusion.100
  273.2 4.3 %fusion.101 = bf16[4,512,128]{2,1,0:T(8,128)(2,1)} fusion(bf16[4,512,128]{2,1,0:T(8,128)(2,1)} %get-tuple-element.349, s32[]{:T(128)} %get-tuple-element.348, bf16[6144,1,128]{2,0,1:T(8,128)(2,1)S(1)} %copy-done.4, f32[512,6144]{1,0:T(8,128)S(1)} %get-tuple-element.310, f32[512]{0:T(512)S(1)} %get-tuple-element.311, ...), kind=kOutput, calls=%fused_computation.14.clone.1 | convolution fusion | flops 821166080 | bytes 14297600 | tf_op jit(solution)/shard_map/while/body/eval_jaxpr/hqk,khd->qhd/dot_general | solution.py:63
  277.5 3.0 fusion.99
  280.6 3.3 fusion.100
  283.9 4.3 %fusion.101 = bf16[4,512,128]{2,1,0:T(8,128)(2,1)} fusion(bf16[4,512,128]{2,1,0:T(8,128)(2,1)} %get-tuple-element.349, s32[]{:T(128)} %get-tuple-element.348, bf16[6144,1,128]{2,0,1:T(8,128)(2,1)S(1)} %copy-done.4, f32[512,6144]{1,0:T(8,128)S(1)} %get-tuple-element.310, f32[512]{0:T(512)S(1)} %get-tuple-element.311, ...), kind=kOutput, calls=%fused_computation.14.clone.1 | convolution fusion | flops 821166080 | bytes 14297600 | tf_op jit(solution)/shard_map/while/body/eval_jaxpr/hqk,khd->qhd/dot_general | solution.py:63
  288.3 40.7 %while.22 = (s32[]{:T(128)}, bf16[4,512,128]{2,1,0:T(8,128)(2,1)S(1)}, pred[6144]{0:T(1024)(128)(4,1)S(1)}, bf16[4,512,1,128]{3,1,2,0:T(8,128)(2,1)}, bf16[6144,...) while((s32[]{:T(128)}, bf16[4,512,128]{2,1,0:T(8,128)(2,1)S(1)}, ...), condition=%wide.region_11.12_spmd, body=%wide.region_8.11_spmd.sunk | while | flops 1651637248 | bytes 47477356 | solution.py:69
  288.5 3.0 fusion.104
  291.5 3.3 fusion.105
  294.8 3.8 fusion.106
  298.6 3.0 fusion.104
  301.6 3.3 fusion.105
  304.9 3.8 fusion.106
  308.7 3.0 fusion.104
  311.7 3.3 fusion.105
  315.0 3.8 fusion.106
  318.8 3.0 fusion.104
  321.9 3.3 fusion.105
  325.1 3.8 fusion.106
  328.9 1.1 maximum_bitcast_fusion
  330.1 8.7 %copy.97 = bf16[1,2,2048,128]{3,1,0,2:T(2,128)(2,1)S(1)} copy(bf16[1,2,2048,128]{3,2,1,0:T(8,128)(2,1)S(1)} %maximum_bitcast_fusion) | data formatting | bytes 2097152 | tf_op jit(solution)/shard_map/broadcast_in_dim | solution.py:117
  338.7 39.5 %all_to_all.66 = bf16[1,2,2048,128]{3,1,0,2:T(2,128)(2,1)S(1)} all-to-all(bf16[1,2,2048,128]{3,1,0,2:T(2,128)(2,1)S(1)} %copy.97), channel_id=1, replica_groups=mesh['branch'=2,'seq'=16,'mp'=8] {'seq'}, dimensions={2} | all-to-all | bytes 2097152 | tf_op jit(solution)/shard_map/all_to_all | solution.py:118
  378.4 0.7 copy.99
  379.1 1.3 copy.100
  (44 shorter events, 2.3 us)
Async XLA Ops:
  10.2 61.6 %all-to-all-start.2 = ((bf16[1,2,128,2048]{2,1,0,3:T(2,128)(2,1)}), bf16[1,2,128,2048]{2,1,0,3:T(2,128)(2,1)S(1)}, u32[]{:S(2)}, u32[]{:S(2)}) async-start(bf16[1,2,128,2048]{2,1,0,3:T(2,128)(2,1)} %copy.89), calls=%async_computation.2 | async-start | bytes 2097152 | tf_op jit(solution)/shard_map/all_to_all | solution.py:82
  20.2 24.7 %collective-permute-start = (bf16[1,2,128,2048]{3,2,1,0:T(8,128)(2,1)}, bf16[1,2,128,2048]{3,2,1,0:T(8,128)(2,1)S(1)}, u32[]{:S(2)}, u32[]{:S(2)}) collective-permute-start(bf16[1,2,128,2048]{3,2,1,0:T(8,128)(2,1)} %param.12), channel_id=1, source_target_pairs={{0,128},{128,0},{1,129},{129,1},{2,130},{130,2},{3,131},{131,3},{4... | collective-permute-start | bytes 3145736 | tf_op jit(solution)/shard_map/ppermute | solution.py:14
  21.5 45.9 %collective-permute-start.1 = (bf16[1,2,128,2048]{3,2,1,0:T(8,128)(2,1)}, bf16[1,2,128,2048]{3,2,1,0:T(8,128)(2,1)S(1)}, u32[]{:S(2)}, u32[]{:S(2)}) collective-permute-start(bf16[1,2,128,2048]{3,2,1,0:T(8,128)(2,1)} %param.13), channel_id=1, source_target_pairs={{0,128},{128,0},{1,129},{129,1},{2,130},{130,2},{3,131},{131,3},{4... | collective-permute-start | bytes 3145736 | tf_op jit(solution)/shard_map/ppermute | solution.py:14
  67.4 45.1 %copy-start.6 = (s32[2]{0:T(128)S(1)}, s32[2]{0:T(128)}, u32[]{:S(2)}) copy-start(s32[2]{0:T(128)} %param.16) | copy-start | bytes 28
  71.8 35.9 %all-to-all-start.1 = ((bf16[1,2,128,2048]{2,1,0,3:T(2,128)(2,1)}), bf16[1,2,128,2048]{2,1,0,3:T(2,128)(2,1)S(1)}, u32[]{:S(2)}, u32[]{:S(2)}) async-start(bf16[1,2,128,2048]{2,1,0,3:T(2,128)(2,1)} %copy.85), calls=%async_computation.1 | async-start | bytes 2097152 | tf_op jit(solution)/shard_map/all_to_all | solution.py:81
  107.7 1.0 copy-start
  108.7 31.4 %all-to-all-start = ((bf16[1,2,128,2048]{2,1,0,3:T(2,128)(2,1)}), bf16[1,2,128,2048]{2,1,0,3:T(2,128)(2,1)S(1)}, u32[]{:S(2)}, u32[]{:S(2)}) async-start(bf16[1,2,128,2048]{2,1,0,3:T(2,128)(2,1)} %copy.83), calls=%async_computation | async-start | bytes 2097152 | tf_op jit(solution)/shard_map/all_to_all | solution.py:80
  112.3 127.7 %all-reduce.5.cloned.1.call-start = ((), (), s32[]{:S(2)}) async-start(), calls=%async_computation.4 | async-start | bytes 4194304 | tf_op jit(solution)/shard_map/psum | solution.py:19
  118.3 7.0 %copy-start.5 = (s32[16,2]{0,1:T(2,128)S(1)}, s32[16,2]{0,1:T(2,128)}, u32[]{:S(2)}) copy-start(s32[16,2]{0,1:T(2,128)} %param.17) | copy-start | bytes 388
  239.9 4.6 %copy-start.1 = (bf16[1,1,16,128,128]{4,3,2,1,0:T(8,128)(2,1)S(1)}, bf16[1,1,16,128,128]{4,3,2,1,0:T(8,128)(2,1)}, u32[]{:S(2)}) copy-start(bf16[1,1,16,128,128]{4,3,2,1,0:T(8,128)(2,1)} %copy.87) | copy-start | bytes 1572868
  239.9 4.6 %copy-start.2 = (bf16[1,1,16,128,128]{4,3,2,1,0:T(8,128)(2,1)S(1)}, bf16[1,1,16,128,128]{4,3,2,1,0:T(8,128)(2,1)}, u32[]{:S(2)}) copy-start(bf16[1,1,16,128,128]{4,3,2,1,0:T(8,128)(2,1)} %copy.94) | copy-start | bytes 1572868
  248.6 3.3 copy-start.4
  259.3 3.3 copy-start.4
  269.9 3.3 copy-start.4
  280.6 3.3 copy-start.4
  291.5 3.3 copy-start.3
  301.6 3.3 copy-start.3
  311.7 3.3 copy-start.3
  321.8 3.3 copy-start.3
Sparse Core Ops, SparseCore 0:
  125.4 114.4 all-reduce.4
where the time goes:
time: 388 us; the launch traced here: 387 us
  waiting for transfers between devices  163 us (42%)
  matrix products  56.5 us (15%)
  other arithmetic  47.9 us (12%)
  blocking collectives  39.5 us (10%)
  local copies, waits for them, and re-layouts  38.3 us (10%)
  starting transfers between devices  23.1 us (6%)
  between operations  18.6 us (5%)
    psum x1, waiting for transfers between devices, from_root(): return lax.psum(block, axis)  97.8 us
    all_to_all x1, blocking collectives, local(): lax.all_to_all(attended, 'seq', split_axis=2, concat_axis=3, tiled=True)  39.5 us
    ppermute x2, waiting for transfers between devices, swapped(): return lax.ppermute(value, axis, pairs)  33.6 us
    dot_general x8, matrix products, one_block(): jnp.einsum('hqk,khd->qhd', rounded, value_whole, preferred_element_type=j...  32.3 us
    reduce_sum x8, other arithmetic, one_block(): totals = jnp.sum(weights, axis=2)  26.3 us
    all_to_all x1, waiting for transfers between devices, local(): lax.all_to_all(mixed_keys, 'seq', split_axis=3, concat_axis=2, tiled=True)  26 us
    dot_general x8, matrix products, score_tile(): jnp.einsum('qhd,khd->hqk', query_block, key_tile, preferred_element_type=...  24.2 us
    all_to_all x1, starting transfers between devices, local(): lax.all_to_all(values, 'seq', split_axis=3, concat_axis=2, tiled=True)  9.97 us
  transfers between devices with their start and end apart: 6, of which 5 were waited for; matrix products, arithmetic and copies ran while one was open for 10% of the time, Pallas kernels for 0%

commit v1 on v0

--- a/solution.py
+++ b/solution.py
@@ -16,7 +16,11 @@
 
 def from_root(block, axis, holder):
     block = jnp.where(lax.axis_index(axis) == holder, block, jnp.zeros_like(block))
-    return lax.psum(block, axis)
+
+    def shape_region(panel, net_axis):
+        return jnp.sum(lax.all_gather(panel, net_axis), 0)
+
+    return shape_region(block, axis)
 
 
 def blend_pair(source, partner, strength):

time: 388 us -> 515 us (1.33)
  waiting for transfers between devices: 163 us -> 261 us
  blocking collectives: 39.5 us -> 68.1 us
  other arithmetic: 47.9 us -> 61 us
  starting transfers between devices: 23.1 us -> 15.4 us
  local copies, waits for them, and re-layouts: 38.3 us -> 33.1 us
    all_gather x0 -> x4, waiting for transfers between devices: none -> 168 us  [shape_region(): return jnp.sum(lax.all_gather(panel, net_axis), 0)]
    psum x1 -> x0, waiting for transfers between devices: 97.8 us -> none  [from_root(): return lax.psum(block, axis)]
    all_to_all x0 -> x1, blocking collectives: none -> 31.5 us  [local(): lax.all_to_all(mixed_keys, 'seq', split_axis=3, concat_axis=2, tiled=True)]
    all_to_all x1 -> x0, waiting for transfers between devices: 26 us -> none  [local(): lax.all_to_all(mixed_keys, 'seq', split_axis=3, concat_axis=2, tiled=True)]
    all_to_all x1, waiting for transfers between devices: 0.01 us -> 21.6 us  [local(): lax.all_to_all(values, 'seq', split_axis=3, concat_axis=2, tiled=True)]
    ppermute x2, waiting for transfers between devices: 33.6 us -> 51 us  [swapped(): return lax.ppermute(value, axis, pairs)]
    all_to_all x1, waiting for transfers between devices: 5.48 us -> 19.4 us  [local(): lax.all_to_all(mixed_queries, 'seq', split_axis=3, concat_axis=2, tiled=T...]
    reduce_sum x0 -> x4, other arithmetic: none -> 12.2 us  [shape_region(): return jnp.sum(lax.all_gather(panel, net_axis), 0)]
  transfers between devices with their start and end apart: 6 -> 8, of which waited for: 5 -> 7; matrix products, arithmetic and copies ran while one was open for 10% -> 8% of each run, Pallas kernels for 0% -> 0%
where the time goes in v1:
time: 515 us; the launch traced here: 514 us
  waiting for transfers between devices  261 us (51%)
  blocking collectives  68.1 us (13%)
  other arithmetic  61 us (12%)
  matrix products  56.6 us (11%)
  local copies, waits for them, and re-layouts  33.1 us (6%)
  between operations  18.4 us (4%)
  starting transfers between devices  15.4 us (3%)
    all_gather x4, waiting for transfers between devices, shape_region(): return jnp.sum(lax.all_gather(panel, net_axis), 0)  168 us
    ppermute x2, waiting for transfers between devices, swapped(): return lax.ppermute(value, axis, pairs)  51 us
    all_to_all x1, blocking collectives, local(): lax.all_to_all(attended, 'seq', split_axis=2, concat_axis=3, tiled=True)  36.7 us
    dot_general x8, matrix products, one_block(): jnp.einsum('hqk,khd->qhd', rounded, value_whole, preferred_element_type=j...  32.4 us
    all_to_all x1, blocking collectives, local(): lax.all_to_all(mixed_keys, 'seq', split_axis=3, concat_axis=2, tiled=True)  31.5 us
    reduce_sum x8, other arithmetic, one_block(): totals = jnp.sum(weights, axis=2)  26.3 us
    dot_general x8, matrix products, score_tile(): jnp.einsum('qhd,khd->hqk', query_block, key_tile, preferred_element_type=...  24.2 us
    all_to_all x1, waiting for transfers between devices, local(): lax.all_to_all(values, 'seq', split_axis=3, concat_axis=2, tiled=True)  21.6 us
  transfers between devices with their start and end apart: 8, of which 7 were waited for; matrix products, arithmetic and copies ran while one was open for 8% of the time, Pallas kernels for 0%

profile of v1, /device:TPU:1, one launch (start us, length us, event | category | flops | bytes accessed | tf_op | source)
XLA Modules:
  0.0 513.9 jit_solution(15154636125270171756)
XLA Ops:
  6.5 3.8 copy.88
  10.3 10.0 %all-to-all-start.2 = ((bf16[1,2,128,2048]{2,1,0,3:T(2,128)(2,1)}), bf16[1,2,128,2048]{2,1,0,3:T(2,128)(2,1)S(1)}, u32[]{:S(2)}, u32[]{:S(2)}) async-start(bf16[1,2,128,2048]{2,1,0,3:T(2,128)(2,1)} %copy.88), calls=%async_computation.2 | async-start | bytes 2097152 | tf_op jit(solution)/shard_map/all_to_all | solution.py:86
  20.3 1.3 fusion.85
  26.7 21.6 %all-to-all-done.2 = bf16[1,2,128,2048]{2,1,0,3:T(2,128)(2,1)S(1)} async-done(((bf16[1,2,128,2048]{2,1,0,3:T(2,128)(2,1)}), bf16[1,2,128,2048]{2,1,0,3:T(2,128)(2,1)S(1)}, u32[]{:S(2)}, u32[]{:S(2)}) %all-to-all-start.2) | async-done | bytes 1048608 | tf_op jit(solution)/shard_map/all_to_all | solution.py:86
  49.1 1.1 dynamic-slice_select_fusion.1
  51.0 1.4 collective-permute-start
  53.3 4.3 compare_select_fusion.1
  57.8 5.7 %broadcast_subtract_fusion = (f32[2048]{0:T(1024)S(1)}, f32[2048]{0:T(1024)S(1)}) fusion(pred[2048]{0:T(1024)(128)(4,1)S(1)} %get-tuple-element.163, pred[2048]{0:T(1024)(128)(4,1)S(1)} %get-tuple-element.162, pred[2048]{0:T(1024)(128)(4,1)S(1)} %get-tuple-element.161, pred[2048]{0:T(1024)(128)(4,1)S(1)} %get-tuple-element.160, ...), kind=kLoop, calls=%fused_computation.76 | loop fusion | flops 38912 | bytes 43044 | tf_op jit(solution)/shard_map/sub | solution.py:28
  63.5 18.7 %collective-permute-done = bf16[1,2,128,2048]{3,2,1,0:T(8,128)(2,1)S(1)} collective-permute-done((bf16[1,2,128,2048]{3,2,1,0:T(8,128)(2,1)}, bf16[1,2,128,2048]{3,2,1,0:T(8,128)(2,1)S(1)}, u32[]{:S(2)}, u32[]{:S(2)}) %collective-permute-start) | collective-permute-done | bytes 1048608 | tf_op jit(solution)/shard_map/ppermute | solution.py:14
  82.2 32.4 %collective-permute-done.1 = bf16[1,2,128,2048]{3,2,1,0:T(8,128)(2,1)S(1)} collective-permute-done((bf16[1,2,128,2048]{3,2,1,0:T(8,128)(2,1)S(1)}, bf16[1,2,128,2048]{3,2,1,0:T(8,128)(2,1)S(1)}, u32[]{:S(2)}, u32[]{:S(2)}) %collective-permute-start.1) | collective-permute-done | bytes 1048608 | tf_op jit(solution)/shard_map/ppermute | solution.py:14
  114.5 3.4 add_convert_fusion
  117.9 0.8 copy.84
  118.7 31.5 %all_to_all.66 = bf16[1,2,128,2048]{2,1,0,3:T(2,128)(2,1)S(1)} all-to-all(bf16[1,2,128,2048]{2,1,0,3:T(2,128)(2,1)S(1)} %copy.84), channel_id=1, replica_groups=mesh['branch'=2,'seq'=16,'mp'=8] {'seq'}, dimensions={3} | all-to-all | bytes 2097152 | tf_op jit(solution)/shard_map/all_to_all | solution.py:85
  151.0 1.1 dynamic-slice_select_fusion.3
  152.7 3.7 copy.82
  156.4 3.7 all-to-all-start
  160.6 1.0 fusion.82
  161.6 2.1 copy.90
  163.7 2.0 copy.94
  165.8 1.0 copy.86
  166.8 1.0 copy.93
  167.9 19.4 %all-to-all-done = bf16[1,2,128,2048]{2,1,0,3:T(2,128)(2,1)S(1)} async-done(((bf16[1,2,128,2048]{2,1,0,3:T(2,128)(2,1)}), bf16[1,2,128,2048]{2,1,0,3:T(2,128)(2,1)S(1)}, u32[]{:S(2)}, u32[]{:S(2)}) %all-to-all-start) | async-done | bytes 1048608 | tf_op jit(solution)/shard_map/all_to_all | solution.py:84
  187.3 0.9 copy.83
  188.2 1.1 fusion.84
  189.3 3.1 reduce_sum.68
  192.3 20.4 %all-gather.11.cloned.1.call-done = bf16[8,2048,128]{2,1,0:T(8,128)(2,1)} async-done(((bf16[1,2048,128]{2,1,0:T(8,128)(2,1)}), bf16[8,2048,128]{2,1,0:T(8,128)(2,1)}) %all-gather.11.cloned.1.call-update) | async-done | bytes 4194320 | tf_op jit(solution)/shard_map/all_gather | solution.py:21
  212.7 3.1 reduce_sum.69
  215.8 1.1 pad_maximum_fusion.5
  216.9 73.2 %all-gather.5.cloned.1.call-done = bf16[8,2048,128]{2,1,0:T(8,128)(2,1)} async-done(((bf16[1,2048,128]{2,1,0:T(8,128)(2,1)}), bf16[8,2048,128]{2,1,0:T(8,128)(2,1)}) %all-gather.5.cloned.1.call-update) | async-done | bytes 4194320 | tf_op jit(solution)/shard_map/all_gather | solution.py:21
  290.0 3.1 reduce_sum.66
  293.1 74.1 %all-gather.7.cloned.1.call-done = bf16[8,2048,128]{2,1,0:T(8,128)(2,1)} async-done(((bf16[1,2048,128]{2,1,0:T(8,128)(2,1)}), bf16[8,2048,128]{2,1,0:T(8,128)(2,1)}) %all-gather.7.cloned.1.call-update) | async-done | bytes 4194320 | tf_op jit(solution)/shard_map/all_gather | solution.py:21
  367.1 3.1 reduce_sum.67
  370.3 4.2 pad_maximum_fusion.1
  374.5 0.9 broadcast.200.clone.1
  375.4 42.6 %while.21 = (s32[]{:T(128)}, bf16[4,512,128]{2,1,0:T(8,128)(2,1)}, pred[6144]{0:T(1024)(128)(4,1)S(1)}, bf16[4,512,1,128]{3,1,2,0:T(8,128)(2,1)}, bf16[6144,1,12...) while((s32[]{:T(128)}, bf16[4,512,128]{2,1,0:T(8,128)(2,1)}, ...), condition=%wide.region_7.8_spmd, body=%wide.region_4.7_spmd.sunk | while | flops 1651637248 | bytes 47477864 | solution.py:73
  375.4 3.0 fusion.99
  378.4 3.3 fusion.100
  381.7 4.3 fusion.101
  386.0 3.0 fusion.99
  389.1 3.3 fusion.100
  392.4 4.3 fusion.101
  396.7 3.0 fusion.99
  399.7 3.3 fusion.100
  403.0 4.3 fusion.101
  407.4 3.0 fusion.99
  410.4 3.3 fusion.100
  413.7 4.3 fusion.101
  418.1 40.7 %while.22 = (s32[]{:T(128)}, bf16[4,512,128]{2,1,0:T(8,128)(2,1)S(1)}, pred[6144]{0:T(1024)(128)(4,1)S(1)}, bf16[4,512,1,128]{3,1,2,0:T(8,128)(2,1)}, bf16[6144,...) while((s32[]{:T(128)}, bf16[4,512,128]{2,1,0:T(8,128)(2,1)S(1)}, ...), condition=%wide.region_11.12_spmd, body=%wide.region_8.11_spmd.sunk | while | flops 1651637248 | bytes 47477356 | solution.py:73
  418.3 3.0 fusion.104
  421.4 3.3 fusion.105
  424.7 3.8 fusion.106
  428.4 3.0 fusion.104
  431.5 3.3 fusion.105
  434.8 3.8 fusion.106
  438.5 3.0 fusion.104
  441.6 3.3 fusion.105
  444.9 3.8 fusion.106
  448.6 3.0 fusion.104
  451.7 3.3 fusion.105
  455.0 3.8 fusion.106
  458.8 1.1 maximum_bitcast_fusion
  459.9 8.7 %copy.96 = bf16[1,2,2048,128]{3,1,0,2:T(2,128)(2,1)S(1)} copy(bf16[1,2,2048,128]{3,2,1,0:T(8,128)(2,1)S(1)} %maximum_bitcast_fusion) | data formatting | bytes 2097152 | tf_op jit(solution)/shard_map/broadcast_in_dim | solution.py:121
  468.6 36.7 %all_to_all.67 = bf16[1,2,2048,128]{3,1,0,2:T(2,128)(2,1)S(1)} all-to-all(bf16[1,2,2048,128]{3,1,0,2:T(2,128)(2,1)S(1)} %copy.96), channel_id=1, replica_groups=mesh['branch'=2,'seq'=16,'mp'=8] {'seq'}, dimensions={2} | all-to-all | bytes 2097152 | tf_op jit(solution)/shard_map/all_to_all | solution.py:122
  506.1 1.3 copy.99
  (52 shorter events, 5.7 us)
Async XLA Ops:
  6.5 45.8 %copy-start.2 = (bf16[1,2,128,2048]{3,2,1,0:T(8,128)(2,1)S(1)}, bf16[1,2,128,2048]{3,2,1,0:T(8,128)(2,1)}, u32[]{:S(2)}) copy-start(bf16[1,2,128,2048]{3,2,1,0:T(8,128)(2,1)} %param.13) | copy-start | bytes 3145732
  6.5 46.0 %copy-start.3 = (f32[1,16]{1,0:T(1,128)S(1)}, f32[1,16]{1,0:T(1,128)}, u32[]{:S(2)}) copy-start(f32[1,16]{1,0:T(1,128)} %param.15) | copy-start | bytes 196
  10.3 38.0 %all-to-all-start.2 = ((bf16[1,2,128,2048]{2,1,0,3:T(2,128)(2,1)}), bf16[1,2,128,2048]{2,1,0,3:T(2,128)(2,1)S(1)}, u32[]{:S(2)}, u32[]{:S(2)}) async-start(bf16[1,2,128,2048]{2,1,0,3:T(2,128)(2,1)} %copy.88), calls=%async_computation.2 | async-start | bytes 2097152 | tf_op jit(solution)/shard_map/all_to_all | solution.py:86
  20.3 169.0 %all-gather.9.cloned.1.call-start = ((), (), s32[]{:S(2)}) async-start(), calls=%async_computation.6 | async-start | bytes 4718592 | tf_op jit(solution)/shard_map/all_gather | solution.py:21
  50.2 162.5 %all-gather.11.cloned.1.call-start = ((), (), s32[]{:S(2)}) async-start(), calls=%async_computation.7 | async-start | bytes 4718592 | tf_op jit(solution)/shard_map/all_gather | solution.py:21
  50.9 239.1 %all-gather.5.cloned.1.call-start = ((), (), s32[]{:S(2)}) async-start(), calls=%async_computation.4 | async-start | bytes 4718592 | tf_op jit(solution)/shard_map/all_gather | solution.py:21
  51.0 31.2 %collective-permute-start = (bf16[1,2,128,2048]{3,2,1,0:T(8,128)(2,1)}, bf16[1,2,128,2048]{3,2,1,0:T(8,128)(2,1)S(1)}, u32[]{:S(2)}, u32[]{:S(2)}) collective-permute-start(bf16[1,2,128,2048]{3,2,1,0:T(8,128)(2,1)} %param.12), channel_id=1, source_target_pairs={{0,128},{128,0},{1,129},{129,1},{2,130},{130,2},{3,131},{131,3},{4... | collective-permute-start | bytes 3145736 | tf_op jit(solution)/shard_map/ppermute | solution.py:14
  52.4 62.2 %collective-permute-start.1 = (bf16[1,2,128,2048]{3,2,1,0:T(8,128)(2,1)S(1)}, bf16[1,2,128,2048]{3,2,1,0:T(8,128)(2,1)S(1)}, u32[]{:S(2)}, u32[]{:S(2)}) collective-permute-start(bf16[1,2,128,2048]{3,2,1,0:T(8,128)(2,1)S(1)} %copy-done.2), channel_id=1, source_target_pairs={{0,128},{128,0},{1,129},{129,1},{2,130},{130,2},{3,131},{131,3},{4... | collective-permute-start | bytes 3145736 | tf_op jit(solution)/shard_map/ppermute | solution.py:14
  150.2 9.9 %copy-start.4 = (s32[16,2]{0,1:T(2,128)S(1)}, s32[16,2]{0,1:T(2,128)}, u32[]{:S(2)}) copy-start(s32[16,2]{0,1:T(2,128)} %param.17) | copy-start | bytes 388
  152.1 215.0 %all-gather.7.cloned.1.call-start = ((), (), s32[]{:S(2)}) async-start(), calls=%async_computation.5 | async-start | bytes 4718592 | tf_op jit(solution)/shard_map/all_gather | solution.py:21
  156.4 30.9 %all-to-all-start = ((bf16[1,2,128,2048]{2,1,0,3:T(2,128)(2,1)}), bf16[1,2,128,2048]{2,1,0,3:T(2,128)(2,1)S(1)}, u32[]{:S(2)}, u32[]{:S(2)}) async-start(bf16[1,2,128,2048]{2,1,0,3:T(2,128)(2,1)} %copy.82), calls=%async_computation | async-start | bytes 2097152 | tf_op jit(solution)/shard_map/all_to_all | solution.py:84
  378.4 3.3 copy-start.1
  389.1 3.3 copy-start.1
  399.7 3.3 copy-start.1
  410.4 3.3 copy-start.1
  421.4 3.3 copy-start
  431.5 3.3 copy-start
  441.6 3.3 copy-start
  451.7 3.3 copy-start
Sparse Core Ops, SparseCore 0:
  50.3 88.9 all-gather.8
  142.0 70.7 all-gather.10
  215.4 74.6 all-gather.4
  292.5 74.6 all-gather.6
